TPU v7x, 32 devices: a whole 2x2x4 slice. The times are simulated.
32 devices in a mesh: row: 8 (over y, x, core), col: 4 (over z).
Axes of the slice: x: 2, y: 2, z: 4, core: 2. Of those that a mesh axis runs over, the one named last changes fastest.
Arguments:
- covariance: float32 [2, 8192, 8192], P(None, 'row', 'col'), as said below
- forcing: float32 [2, 8192, 8192], P(None, 'row', 'col'), as said below
- coupling: float32 [2, 64, 64], replicated, may hold values from -0.5 to 0.5
- vertical: float32 [2, 128, 128], replicated, may hold values from -0.375 to 0.375
- damping: float32 [64, 128], replicated, may hold values from 0.3 to 3
- advection: float32 [64, 128], replicated, may hold values from -2 to 2
Outputs:
- advanced: float32 [2, 8192, 8192], P(None, 'row', 'col')
Inputs may be any that keep to these rules, and one draw needn't show every extreme that they name: The covariance equals its conjugate transpose: the real plane is symmetric, the imaginary plane antisymmetric. The forcing equals its conjugate transpose: the real plane is symmetric, the imaginary plane antisymmetric.
All inputs are finite; a program needn't handle non-finite values.
Results may differ from a plain program's by a relative error of at most 0.000073.
Values sent between devices are 32-bit elements; how exact they have to be, the bound alone decides.
A program may use at most 320 MiB of HBM per device.

v0:
```python
import jax
import jax.numpy as jnp
from jax import lax
from jax.sharding import PartitionSpec as P

step_size = 0.25


def complex_einsum(pattern, factor, values):

    def single(factor_part, value_part):
        return jnp.einsum(pattern, factor_part, value_part, precision=lax.Precision.HIGHEST)

    real_part = single(factor[0], values[0]) - single(factor[1], values[1])
    imag_part = single(factor[0], values[1]) + single(factor[1], values[0])
    return jnp.stack([real_part, imag_part])


def complex_scale(factor, values):
    real_part = factor[0] * values[0] - factor[1] * values[1]
    imag_part = factor[0] * values[1] + factor[1] * values[0]
    return jnp.stack([real_part, imag_part])


def conjugate(values):
    return jnp.stack([values[0], -values[1]])


def left_apply(by_rows, coupling, vertical, rates):
    total = complex_einsum("lm,amj->alj", vertical, by_rows)
    total = total + complex_einsum("ab,blj->alj", coupling, by_rows)
    return total + complex_scale(rates[:, :, :, None], by_rows)


def right_apply(by_cols, coupling, vertical, rates):
    total = complex_einsum("lm,iam->ial", conjugate(vertical), by_cols)
    total = total + complex_einsum("ab,ibl->ial", conjugate(coupling), by_cols)
    return total + complex_scale(conjugate(rates)[:, None], by_cols)


def tendency(block_tile, forcing, coupling, vertical, rates):
    rows_here = block_tile.shape[1]
    cols_here = block_tile.shape[2]
    levels = vertical.shape[1]
    lats_row = rows_here // levels
    lats_col = cols_here // levels
    by_rows = block_tile.reshape(2, lats_row, levels, cols_here)
    regrouped = lax.all_to_all(by_rows, "row", split_axis=3, concat_axis=1, tiled=True)
    applied = left_apply(regrouped, coupling, vertical, rates)
    left_term = lax.all_to_all(applied, "row", split_axis=1, concat_axis=3, tiled=True)
    left_term = left_term.reshape(2, rows_here, cols_here)
    by_cols = block_tile.reshape(2, rows_here, lats_col, levels)
    regrouped_cols = lax.all_to_all(by_cols, "col", split_axis=1, concat_axis=2, tiled=True)
    applied_cols = right_apply(regrouped_cols, coupling, vertical, rates)
    right_term = lax.all_to_all(
        applied_cols, "col", split_axis=2, concat_axis=1, tiled=True
    ).reshape(2, rows_here, cols_here)
    return left_term + right_term + forcing


def shards(covariance, forcing, coupling, vertical, damping, advection):
    rates = jnp.stack([-damping, advection])
    first_rate = tendency(covariance, forcing, coupling, vertical, rates)
    midpoint = covariance + 0.5 * step_size * first_rate
    return covariance + step_size * tendency(midpoint, forcing, coupling, vertical, rates)


def solution(mesh):
    return jax.shard_map(
        shards,
        mesh=mesh,
        in_specs=(P(None, "row", "col"), P(None, "row", "col"), P(), P(), P(), P()),
        out_specs=P(None, "row", "col"),
        check_vma=False,
    )
```

profile of v0, /device:TPU:0, one launch (start us, length us, event | category | flops | bytes accessed | tf_op | source)
XLA Modules:
  0.0 2441.1 jit_solution(17442187832632348149)
XLA Ops:
  0.0 17.6 copy.149
  39.9 168.1 %all-to-all-done = f32[2,8,128,2048]{2,1,0,3:T(8,128)} async-done(((f32[2,8,128,2048]{2,1,0,3:T(8,128)}), f32[2,8,128,2048]{2,1,0,3:T(8,128)}, u32[]{:S(2)}, u32[]{:S(2)}) %all-to-all-start) | async-done | bytes 16777248 | tf_op jit(solution)/shard_map/all_to_all | solution.py:48
  397.3 19.0 add_bitcast_fusion.4
  439.1 137.1 %all-to-all-done.2 = f32[2,1024,16,128]{3,2,0,1:T(8,128)} async-done(((f32[2,1024,16,128]{3,2,0,1:T(8,128)}), f32[2,1024,16,128]{3,2,0,1:T(8,128)}, u32[]{:S(2)}, u32[]{:S(2)}) %all-to-all-start.2) | async-done | bytes 16777248 | tf_op jit(solution)/shard_map/all_to_all | solution.py:53
  641.2 17.4 fusion.20
  720.1 41.0 %fusion.6 = (f32[1,256,64,128]{3,1,2,0:T(8,128)}, f32[1,256,64,128]{3,1,2,0:T(8,128)}) fusion(f32[256,128,64]{1,2,0:T(8,128)} %fusion.20, f32[256,128,64]{1,2,0:T(8,128)} %fusion.16, f32[256,128,64]{1,2,0:T(8,128)} %fusion.18, f32[256,128,64]{1,2,0:T(8,128)} %fusion.22), kind=kLoop, calls=%fused_computation.16 | loop fusion | flops 4194304 | bytes 50331648 | tf_op jit(solution)/shard_map/stack | solution.py:16
  791.0 17.4 copy.164
  808.4 18.0 reshape.251
  826.3 328.4 %all-to-all-done.3 = f32[2,256,64,128]{3,1,0,2:T(8,128)} async-done(((f32[2,256,64,128]{3,1,0,2:T(8,128)}), f32[2,256,64,128]{3,1,0,2:T(8,128)}, u32[]{:S(2)}, u32[]{:S(2)}) %all-to-all-start.3) | async-done | bytes 16777248 | tf_op jit(solution)/shard_map/all_to_all | solution.py:55
  1154.7 17.8 copy.249
  1172.5 18.0 reshape.253
  1190.4 29.2 %multiply_add_fusion.1 = f32[2,1024,2048]{2,1,0:T(8,128)} fusion(f32[2,1024,2048]{2,1,0:T(8,128)} %param.6, f32[2,1024,2048]{2,1,0:T(8,128)} %param.7, f32[2,1024,2048]{2,1,0:T(8,128)} %reshape.251, f32[2,1024,2048]{2,1,0:T(8,128)} %reshape.253), kind=kLoop, calls=%fused_computation.10 | loop fusion | flops 16777216 | bytes 83886080 | tf_op jit(solution)/shard_map/add | solution.py:64
  1219.6 17.7 copy.181
  1259.5 167.4 %all-to-all-done.4 = f32[2,8,128,2048]{2,1,0,3:T(8,128)} async-done(((f32[2,8,128,2048]{2,1,0,3:T(8,128)}), f32[2,8,128,2048]{2,1,0,3:T(8,128)}, u32[]{:S(2)}, u32[]{:S(2)}) %all-to-all-start.4) | async-done | bytes 16777248 | tf_op jit(solution)/shard_map/all_to_all | solution.py:48
  1659.0 135.3 %all-to-all-done.6 = f32[2,1024,16,128]{3,2,0,1:T(8,128)} async-done(((f32[2,1024,16,128]{3,2,0,1:T(8,128)}), f32[2,1024,16,128]{3,2,0,1:T(8,128)}, u32[]{:S(2)}, u32[]{:S(2)}) %all-to-all-start.6) | async-done | bytes 16777248 | tf_op jit(solution)/shard_map/all_to_all | solution.py:53
  1845.3 17.4 fusion.12
  1934.3 18.2 fusion.5
  1952.6 18.4 fusion.4
  2012.2 17.4 copy.196
  2029.6 18.0 reshape.255
  2047.5 328.4 %all-to-all-done.7 = f32[2,256,64,128]{3,1,0,2:T(8,128)} async-done(((f32[2,256,64,128]{3,1,0,2:T(8,128)}), f32[2,256,64,128]{3,1,0,2:T(8,128)}, u32[]{:S(2)}, u32[]{:S(2)}) %all-to-all-start.7) | async-done | bytes 16777248 | tf_op jit(solution)/shard_map/all_to_all | solution.py:55
  2375.9 17.8 copy.212
  2393.7 18.0 reshape.257
  2411.7 29.2 %multiply_add_fusion = f32[2,1024,2048]{2,1,0:T(8,128)} fusion(f32[2,1024,2048]{2,1,0:T(8,128)} %param.6, f32[2,1024,2048]{2,1,0:T(8,128)} %param.7, f32[2,1024,2048]{2,1,0:T(8,128)} %reshape.255, f32[2,1024,2048]{2,1,0:T(8,128)} %reshape.257), kind=kLoop, calls=%fused_computation.9 | loop fusion | flops 16777216 | bytes 83886080 | tf_op jit(solution)/shard_map/add | solution.py:65
  (136 shorter events, 808.5 us)
Async XLA Ops:
  17.6 190.4 %all-to-all-start = ((f32[2,8,128,2048]{2,1,0,3:T(8,128)}), f32[2,8,128,2048]{2,1,0,3:T(8,128)}, u32[]{:S(2)}, u32[]{:S(2)}) async-start(f32[2,8,128,2048]{2,1,0,3:T(8,128)} %copy.149), calls=%async_computation | async-start | bytes 33554432 | tf_op jit(solution)/shard_map/all_to_all | solution.py:48
  39.9 175.3 %copy-start.13 = (f32[64,128]{1,0:T(8,128)S(1)}, f32[64,128]{1,0:T(8,128)}, u32[]{:S(2)}) copy-start(f32[64,128]{1,0:T(8,128)} %param.10) | copy-start | bytes 98308
  208.0 368.2 %all-to-all-start.2 = ((f32[2,1024,16,128]{3,2,0,1:T(8,128)}), f32[2,1024,16,128]{3,2,0,1:T(8,128)}, u32[]{:S(2)}, u32[]{:S(2)}) async-start(f32[2,1024,16,128]{3,2,0,1:T(8,128)} %copy.213), calls=%async_computation.2 | async-start | bytes 33554432 | tf_op jit(solution)/shard_map/all_to_all | solution.py:53
  215.2 497.9 %copy-start.7 = (f32[64,128]{1,0:T(8,128)}, f32[64,128]{1,0:T(8,128)S(1)}, u32[]{:S(2)}) copy-start(f32[64,128]{1,0:T(8,128)S(1)} %neg.27) | copy-start | bytes 98308
  349.3 20.4 slice-start.6
  349.3 31.2 %slice-start.4 = ((s8[8388608]{0:T(1024)(128)(4,1)}), s8[4194304]{0:T(1024)(128)(4,1)S(1)}, s32[]{:S(2)}) async-start(s8[8388608]{0:T(1024)(128)(4,1)} %bitcast.244), calls=%async_computation.12 | async-start | bytes 8388608
  360.4 20.2 slice-start.5
  380.6 9.6 copy-start.9
  576.2 207.7 %all-to-all-start.1 = ((f32[2,64,128,256]{2,3,0,1:T(8,128)}), f32[2,64,128,256]{2,3,0,1:T(8,128)}, u32[]{:S(2)}, u32[]{:S(2)}) async-start(f32[2,64,128,256]{2,3,0,1:T(8,128)} %copy.163), calls=%async_computation.1 | async-start | bytes 33554432 | tf_op jit(solution)/shard_map/all_to_all | solution.py:50
  582.2 130.9 %copy-start.11 = (f32[64,128]{1,0:T(8,128)}, f32[64,128]{1,0:T(8,128)S(1)}, u32[]{:S(2)}) copy-start(f32[64,128]{1,0:T(8,128)S(1)} %neg.32) | copy-start | bytes 98308
  784.0 370.8 %all-to-all-start.3 = ((f32[2,256,64,128]{3,1,0,2:T(8,128)}), f32[2,256,64,128]{3,1,0,2:T(8,128)}, u32[]{:S(2)}, u32[]{:S(2)}) async-start(f32[2,256,64,128]{3,1,0,2:T(8,128)} %copy.179), calls=%async_computation.3 | async-start | bytes 33554432 | tf_op jit(solution)/shard_map/all_to_all | solution.py:55
  1237.3 189.7 %all-to-all-start.4 = ((f32[2,8,128,2048]{2,1,0,3:T(8,128)}), f32[2,8,128,2048]{2,1,0,3:T(8,128)}, u32[]{:S(2)}, u32[]{:S(2)}) async-start(f32[2,8,128,2048]{2,1,0,3:T(8,128)} %copy.181), calls=%async_computation.4 | async-start | bytes 33554432 | tf_op jit(solution)/shard_map/all_to_all | solution.py:48
  1426.9 367.4 %all-to-all-start.6 = ((f32[2,1024,16,128]{3,2,0,1:T(8,128)}), f32[2,1024,16,128]{3,2,0,1:T(8,128)}, u32[]{:S(2)}, u32[]{:S(2)}) async-start(f32[2,1024,16,128]{3,2,0,1:T(8,128)} %copy.197), calls=%async_computation.6 | async-start | bytes 33554432 | tf_op jit(solution)/shard_map/all_to_all | solution.py:53
  1565.3 18.7 slice-start.2
  1565.3 27.8 %slice-start = ((s8[8388608]{0:T(1024)(128)(4,1)}), s8[4194304]{0:T(1024)(128)(4,1)S(1)}, s32[]{:S(2)}) async-start(s8[8388608]{0:T(1024)(128)(4,1)} %bitcast.233), calls=%async_computation.8 | async-start | bytes 8388608
  1574.7 9.4 slice-start.3
  1574.7 18.5 slice-start.1
  1613.6 11.3 copy-start.8
  1613.6 11.3 copy-start.10
  1794.3 210.6 %all-to-all-start.5 = ((f32[2,64,128,256]{2,3,0,1:T(8,128)}), f32[2,64,128,256]{2,3,0,1:T(8,128)}, u32[]{:S(2)}, u32[]{:S(2)}) async-start(f32[2,64,128,256]{2,3,0,1:T(8,128)} %copy.195), calls=%async_computation.5 | async-start | bytes 33554432 | tf_op jit(solution)/shard_map/all_to_all | solution.py:50
  1819.1 106.0 %copy-start = (f32[1,256,4,16,128]{4,1,3,2,0:T(8,128)}, f32[1,256,4,16,128]{4,1,3,2,0:T(8,128)S(1)}, u32[]{:S(2)}) copy-start(f32[1,256,4,16,128]{4,1,3,2,0:T(8,128)S(1)} %copy.199) | copy-start | bytes 25165828
  1828.1 86.1 %copy-start.1 = (f32[1,256,4,16,128]{4,1,3,2,0:T(8,128)}, f32[1,256,4,16,128]{4,1,3,2,0:T(8,128)S(1)}, u32[]{:S(2)}) copy-start(f32[1,256,4,16,128]{4,1,3,2,0:T(8,128)S(1)} %copy.200) | copy-start | bytes 25165828
  1952.6 18.4 copy-start.12
  2004.9 371.0 %all-to-all-start.7 = ((f32[2,256,64,128]{3,1,0,2:T(8,128)}), f32[2,256,64,128]{3,1,0,2:T(8,128)}, u32[]{:S(2)}, u32[]{:S(2)}) async-start(f32[2,256,64,128]{3,1,0,2:T(8,128)} %copy.211), calls=%async_computation.7 | async-start | bytes 33554432 | tf_op jit(solution)/shard_map/all_to_all | solution.py:55
  (6 other events, 54.1 us)
where the time goes:
time: 2450 us; the launch traced here: 2440 us
  waiting for transfers between devices  1260 us (51%)
  local copies, waits for them, and re-layouts  457 us (19%)
  matrix products  386 us (16%)
  other arithmetic  281 us (11%)
  starting transfers between devices  52 us (2%)
    all_to_all x2, waiting for transfers between devices, tendency(): lax.all_to_all(applied_cols, 'col', split_axis=2, concat_axis=1, tiled=True)  657 us
    dot_general x32, matrix products, single(): jnp.einsum(pattern, factor_part, value_part, precision=lax.Precision.HIGH...  386 us
    all_to_all x2, waiting for transfers between devices, tendency(): lax.all_to_all(by_rows, 'row', split_axis=3, concat_axis=1, tiled=True)  336 us
    all_to_all x2, waiting for transfers between devices, tendency(): lax.all_to_all(by_cols, 'col', split_axis=1, concat_axis=2, tiled=True)  272 us
    another operation x6, other arithmetic, complex_einsum(): return jnp.stack([real_part, imag_part])  119 us
    slice x12, local copies, waits for them, and re-layouts, complex_einsum(): real_part = single(factor[0], values[0]) - single(factor[1], values[1])  79.4 us
    dot_general x8, local copies, waits for them, and re-layouts, single(): jnp.einsum(pattern, factor_part, value_part, precision=lax.Precision.HIGH...  74.2 us
  transfers between devices with their start and end apart: 8, of which 6 were waited for; matrix products, arithmetic and copies ran while one was open for 39% of the time, Pallas kernels for 0%

commit v1 on v0

--- a/solution.py
+++ b/solution.py
@@ -2,6 +2,7 @@
 import jax.numpy as jnp
 from jax import lax
 from jax.sharding import PartitionSpec as P
+from jax.lax import axis_index, ppermute, psum
 
 step_size = 0.25
 
@@ -45,7 +46,23 @@
     lats_row = rows_here // levels
     lats_col = cols_here // levels
     by_rows = block_tile.reshape(2, lats_row, levels, cols_here)
-    regrouped = lax.all_to_all(by_rows, "row", split_axis=3, concat_axis=1, tiled=True)
+    h_now, local_next = (psum(1, "row"), axis_index("row"))
+    arr_next = by_rows.shape[3] // h_now
+    top = list(by_rows.shape)
+    top[3] = arr_next
+    current_block = top[1]
+    top[1] = current_block * h_now
+    regrouped = jnp.zeros(top, by_rows.dtype)
+    for k in range(h_now):
+        fresh = lax.dynamic_slice_in_dim(by_rows, (local_next ^ k) * arr_next, arr_next, axis=3)
+        if k:
+            copies = []
+            for p in range(h_now):
+                copies.append((p, p ^ k))
+            fresh = ppermute(fresh, "row", copies)
+        regrouped = lax.dynamic_update_slice_in_dim(
+            regrouped, fresh, (local_next ^ k) * current_block, axis=1
+        )
     applied = left_apply(regrouped, coupling, vertical, rates)
     left_term = lax.all_to_all(applied, "row", split_axis=1, concat_axis=3, tiled=True)
     left_term = left_term.reshape(2, rows_here, cols_here)

time: 2450 us -> 2200 us (0.90)
  waiting for transfers between devices: 1260 us -> 944 us
  local copies, waits for them, and re-layouts: 457 us -> 495 us
    all_to_all x2 -> x0, waiting for transfers between devices: 336 us -> none  [tendency(): lax.all_to_all(by_rows, 'row', split_axis=3, concat_axis=1, tiled=True)]
    ppermute x0 -> x14, waiting for transfers between devices: none -> 287 us  [tendency(): fresh = ppermute(fresh, 'row', copies)]
    all_to_all x2, waiting for transfers between devices: 272 us -> 0.01 us  [tendency(): lax.all_to_all(by_cols, 'col', split_axis=1, concat_axis=2, tiled=True)]
    dynamic_update_slice x0 -> x16, local copies, waits for them, and re-layouts: none -> 46.5 us  [tendency(): lax.dynamic_update_slice_in_dim(regrouped, fresh, (local_next ^ k) * curr...]
    unnamed x46 -> x52, local copies, waits for them, and re-layouts: 18.9 us -> 63.4 us
    slice x12 -> x6, local copies, waits for them, and re-layouts: 79.4 us -> 39.4 us  [complex_einsum(): real_part = single(factor[0], values[0]) - single(factor[1], values[1])]
    reshape x2 -> x0, local copies, waits for them, and re-layouts: 35.3 us -> none  [tendency(): by_rows = block_tile.reshape(2, lats_row, levels, cols_here)]
  transfers between devices with their start and end apart: 8 -> 20, of which waited for: 6 -> 8; matrix products, arithmetic and copies ran while one was open for 39% -> 47% of each run, Pallas kernels for 0% -> 0%
where the time goes in v1:
time: 2200 us; the launch traced here: 2180 us
  waiting for transfers between devices  944 us (43%)
  local copies, waits for them, and re-layouts  495 us (22%)
  matrix products  390 us (18%)
  other arithmetic  296 us (13%)
  starting transfers between devices  58.1 us (3%)
    all_to_all x2, waiting for transfers between devices, tendency(): lax.all_to_all(applied_cols, 'col', split_axis=2, concat_axis=1, tiled=True)  657 us
    dot_general x32, matrix products, single(): jnp.einsum(pattern, factor_part, value_part, precision=lax.Precision.HIGH...  390 us
    ppermute x14, waiting for transfers between devices, tendency(): fresh = ppermute(fresh, 'row', copies)  287 us
    another operation x6, other arithmetic, complex_einsum(): return jnp.stack([real_part, imag_part])  119 us
    dot_general x8, local copies, waits for them, and re-layouts, single(): jnp.einsum(pattern, factor_part, value_part, precision=lax.Precision.HIGH...  74.6 us
    unnamed x52, local copies, waits for them, and re-layouts  63.4 us
    sub x4, other arithmetic, complex_scale(): real_part = factor[0] * values[0] - factor[1] * values[1]  52 us
    dynamic_update_slice x16, local copies, waits for them, and re-layouts, tendency(): lax.dynamic_update_slice_in_dim(regrouped, fresh, (local_next ^ k) * curr...  46.5 us
  transfers between devices with their start and end apart: 20, of which 8 were waited for; matrix products, arithmetic and copies ran while one was open for 47% of the time, Pallas kernels for 0%

profile of v1, /device:TPU:0, one launch (start us, length us, event | category | flops | bytes accessed | tf_op | source)
XLA Modules:
  0.0 2184.3 jit_solution(3030562245335714981)
XLA Ops:
  63.0 27.8 %collective-permute-done.1 = f32[2,8,128,256]{2,3,1,0:T(8,128)} collective-permute-done((f32[2,8,128,256]{2,3,1,0:T(8,128)}, f32[2,8,128,256]{2,3,1,0:T(8,128)}, u32[]{:S(2)}, u32[]{:S(2)}) %collective-permute-start.1) | collective-permute-done | bytes 2097184 | tf_op jit(solution)/shard_map/ppermute | solution.py:62
  110.4 24.9 %collective-permute-done.2 = f32[2,8,128,256]{2,3,1,0:T(8,128)} collective-permute-done((f32[2,8,128,256]{2,3,1,0:T(8,128)}, f32[2,8,128,256]{2,3,1,0:T(8,128)}, u32[]{:S(2)}, u32[]{:S(2)}) %collective-permute-start.2) | collective-permute-done | bytes 2097184 | tf_op jit(solution)/shard_map/ppermute | solution.py:62
  141.6 90.7 %collective-permute-done.4 = f32[2,8,128,256]{2,3,1,0:T(8,128)} collective-permute-done((f32[2,8,128,256]{2,3,1,0:T(8,128)}, f32[2,8,128,256]{2,3,1,0:T(8,128)}, u32[]{:S(2)}, u32[]{:S(2)}) %collective-permute-start.4) | collective-permute-done | bytes 2097184 | tf_op jit(solution)/shard_map/ppermute | solution.py:62
  403.3 19.0 add_bitcast_fusion.4
  527.7 17.4 fusion.22
  589.3 41.0 %fusion.6 = (f32[1,256,64,128]{3,1,2,0:T(8,128)}, f32[1,256,64,128]{3,1,2,0:T(8,128)}) fusion(f32[256,128,64]{1,2,0:T(8,128)} %fusion.20, f32[256,128,64]{1,2,0:T(8,128)} %fusion.16, f32[256,128,64]{1,2,0:T(8,128)} %fusion.18, f32[256,128,64]{1,2,0:T(8,128)} %fusion.22), kind=kLoop, calls=%fused_computation.16 | loop fusion | flops 4194304 | bytes 50331648 | tf_op jit(solution)/shard_map/stack | solution.py:17
  660.1 17.4 copy.120
  677.5 18.0 reshape.151
  695.5 328.6 %all-to-all-done.2 = f32[2,256,64,128]{3,1,0,2:T(8,128)} async-done(((f32[2,256,64,128]{3,1,0,2:T(8,128)}), f32[2,256,64,128]{3,1,0,2:T(8,128)}, u32[]{:S(2)}, u32[]{:S(2)}) %all-to-all-start.2) | async-done | bytes 16777248 | tf_op jit(solution)/shard_map/all_to_all | solution.py:72
  1024.1 17.8 copy.223
  1041.8 18.0 reshape.153
  1059.8 29.2 %multiply_add_fusion.1 = f32[2,1024,2048]{2,1,0:T(8,128)} fusion(f32[2,1024,2048]{2,1,0:T(8,128)} %param.6, f32[2,1024,2048]{2,1,0:T(8,128)} %param.7, f32[2,1024,2048]{2,1,0:T(8,128)} %reshape.151, f32[2,1024,2048]{2,1,0:T(8,128)} %reshape.153), kind=kLoop, calls=%fused_computation.10 | loop fusion | flops 16777216 | bytes 83886080 | tf_op jit(solution)/shard_map/add | solution.py:81
  1151.4 27.8 %collective-permute-done.8 = f32[2,8,128,256]{2,3,1,0:T(8,128)} collective-permute-done((f32[2,8,128,256]{2,3,1,0:T(8,128)}, f32[2,8,128,256]{2,3,1,0:T(8,128)}, u32[]{:S(2)}, u32[]{:S(2)}) %collective-permute-start.8) | collective-permute-done | bytes 2097184 | tf_op jit(solution)/shard_map/ppermute | solution.py:62
  1198.6 25.1 %collective-permute-done.9 = f32[2,8,128,256]{2,3,1,0:T(8,128)} collective-permute-done((f32[2,8,128,256]{2,3,1,0:T(8,128)}, f32[2,8,128,256]{2,3,1,0:T(8,128)}, u32[]{:S(2)}, u32[]{:S(2)}) %collective-permute-start.9) | collective-permute-done | bytes 2097184 | tf_op jit(solution)/shard_map/ppermute | solution.py:62
  1229.9 90.4 %collective-permute-done.11 = f32[2,8,128,256]{2,3,1,0:T(8,128)} collective-permute-done((f32[2,8,128,256]{2,3,1,0:T(8,128)}, f32[2,8,128,256]{2,3,1,0:T(8,128)}, u32[]{:S(2)}, u32[]{:S(2)}) %collective-permute-start.11) | collective-permute-done | bytes 2097184 | tf_op jit(solution)/shard_map/ppermute | solution.py:62
  1570.8 17.4 fusion.14
  1677.2 18.2 fusion.5
  1695.4 18.4 fusion.4
  1754.9 17.4 copy.154
  1772.3 18.0 reshape.155
  1790.3 328.6 %all-to-all-done.5 = f32[2,256,64,128]{3,1,0,2:T(8,128)} async-done(((f32[2,256,64,128]{3,1,0,2:T(8,128)}), f32[2,256,64,128]{3,1,0,2:T(8,128)}, u32[]{:S(2)}, u32[]{:S(2)}) %all-to-all-start.5) | async-done | bytes 16777248 | tf_op jit(solution)/shard_map/all_to_all | solution.py:72
  2118.9 17.8 copy.170
  2136.7 18.0 reshape.157
  2154.7 29.2 %multiply_add_fusion = f32[2,1024,2048]{2,1,0:T(8,128)} fusion(f32[2,1024,2048]{2,1,0:T(8,128)} %param.6, f32[2,1024,2048]{2,1,0:T(8,128)} %param.7, f32[2,1024,2048]{2,1,0:T(8,128)} %reshape.155, f32[2,1024,2048]{2,1,0:T(8,128)} %reshape.157), kind=kLoop, calls=%fused_computation.9 | loop fusion | flops 16777216 | bytes 83886080 | tf_op jit(solution)/shard_map/add | solution.py:82
  (172 shorter events, 907.4 us)
Async XLA Ops:
  16.5 428.8 %all-to-all-start.1 = ((f32[2,1024,16,128]{3,2,0,1:T(8,128)}), f32[2,1024,16,128]{3,2,0,1:T(8,128)}, u32[]{:S(2)}, u32[]{:S(2)}) async-start(f32[2,1024,16,128]{3,2,0,1:T(8,128)} %copy.171), calls=%async_computation.1 | async-start | bytes 33554432 | tf_op jit(solution)/shard_map/all_to_all | solution.py:70
  38.0 19.4 collective-permute-start
  41.5 49.3 %collective-permute-start.1 = (f32[2,8,128,256]{2,3,1,0:T(8,128)}, f32[2,8,128,256]{2,3,1,0:T(8,128)}, u32[]{:S(2)}, u32[]{:S(2)}) collective-permute-start(f32[2,8,128,256]{2,3,1,0:T(8,128)} %copy.174), channel_id=1, source_target_pairs={{0,8},{4,12},{8,0},{12,4},{16,24},{20,28},{24,16},{28,20},{1,9},{5... | collective-permute-start | bytes 6291464 | tf_op jit(solution)/shard_map/ppermute | solution.py:62
  46.9 88.5 %collective-permute-start.2 = (f32[2,8,128,256]{2,3,1,0:T(8,128)}, f32[2,8,128,256]{2,3,1,0:T(8,128)}, u32[]{:S(2)}, u32[]{:S(2)}) collective-permute-start(f32[2,8,128,256]{2,3,1,0:T(8,128)} %copy.175), channel_id=1, source_target_pairs={{0,12},{4,8},{8,4},{12,0},{16,28},{20,24},{24,20},{28,16},{1,13},{... | collective-permute-start | bytes 6291464 | tf_op jit(solution)/shard_map/ppermute | solution.py:62
  49.9 88.5 %collective-permute-start.3 = (f32[2,8,128,256]{2,3,1,0:T(8,128)}, f32[2,8,128,256]{2,3,1,0:T(8,128)}, u32[]{:S(2)}, u32[]{:S(2)}) collective-permute-start(f32[2,8,128,256]{2,3,1,0:T(8,128)} %copy.176), channel_id=1, source_target_pairs={{0,16},{4,20},{8,24},{12,28},{16,0},{20,4},{24,8},{28,12},{1,17},{... | collective-permute-start | bytes 6291464 | tf_op jit(solution)/shard_map/ppermute | solution.py:62
  54.6 177.6 %collective-permute-start.4 = (f32[2,8,128,256]{2,3,1,0:T(8,128)}, f32[2,8,128,256]{2,3,1,0:T(8,128)}, u32[]{:S(2)}, u32[]{:S(2)}) collective-permute-start(f32[2,8,128,256]{2,3,1,0:T(8,128)} %copy.177), channel_id=1, source_target_pairs={{0,20},{4,16},{8,28},{12,24},{16,4},{20,0},{24,12},{28,8},{1,21},{... | collective-permute-start | bytes 6291464 | tf_op jit(solution)/shard_map/ppermute | solution.py:62
  57.5 177.8 %collective-permute-start.5 = (f32[2,8,128,256]{2,3,1,0:T(8,128)}, f32[2,8,128,256]{2,3,1,0:T(8,128)}, u32[]{:S(2)}, u32[]{:S(2)}) collective-permute-start(f32[2,8,128,256]{2,3,1,0:T(8,128)} %copy.178), channel_id=1, source_target_pairs={{0,24},{4,28},{8,16},{12,20},{16,8},{20,12},{24,0},{28,4},{1,25},{... | collective-permute-start | bytes 6291464 | tf_op jit(solution)/shard_map/ppermute | solution.py:62
  90.7 147.7 %collective-permute-start.6 = (f32[2,8,128,256]{2,3,1,0:T(8,128)}, f32[2,8,128,256]{2,3,1,0:T(8,128)}, u32[]{:S(2)}, u32[]{:S(2)}) collective-permute-start(f32[2,8,128,256]{2,3,1,0:T(8,128)} %copy.179), channel_id=1, source_target_pairs={{0,28},{4,24},{8,20},{12,16},{16,12},{20,8},{24,4},{28,0},{1,29},{... | collective-permute-start | bytes 6291464 | tf_op jit(solution)/shard_map/ppermute | solution.py:62
  94.4 147.2 %copy-start.8 = (f32[64,128]{1,0:T(8,128)}, f32[64,128]{1,0:T(8,128)S(1)}, u32[]{:S(2)}) copy-start(f32[64,128]{1,0:T(8,128)S(1)} %neg.27) | copy-start | bytes 98308
  138.4 103.1 %copy-start.12 = (f32[64,128]{1,0:T(8,128)S(1)}, f32[64,128]{1,0:T(8,128)}, u32[]{:S(2)}) copy-start(f32[64,128]{1,0:T(8,128)} %param.11) | copy-start | bytes 98308
  445.2 207.8 %all-to-all-start = ((f32[2,64,128,256]{2,3,0,1:T(8,128)}), f32[2,64,128,256]{2,3,0,1:T(8,128)}, u32[]{:S(2)}, u32[]{:S(2)}) async-start(f32[2,64,128,256]{2,3,0,1:T(8,128)} %copy.119), calls=%async_computation | async-start | bytes 33554432 | tf_op jit(solution)/shard_map/all_to_all | solution.py:67
  451.5 130.8 %copy-start.14 = (f32[64,128]{1,0:T(8,128)}, f32[64,128]{1,0:T(8,128)S(1)}, u32[]{:S(2)}) copy-start(f32[64,128]{1,0:T(8,128)S(1)} %neg.32) | copy-start | bytes 98308
  653.1 371.0 %all-to-all-start.2 = ((f32[2,256,64,128]{3,1,0,2:T(8,128)}), f32[2,256,64,128]{3,1,0,2:T(8,128)}, u32[]{:S(2)}, u32[]{:S(2)}) async-start(f32[2,256,64,128]{3,1,0,2:T(8,128)} %copy.135), calls=%async_computation.2 | async-start | bytes 33554432 | tf_op jit(solution)/shard_map/all_to_all | solution.py:72
  1105.5 431.5 %all-to-all-start.4 = ((f32[2,1024,16,128]{3,2,0,1:T(8,128)}), f32[2,1024,16,128]{3,2,0,1:T(8,128)}, u32[]{:S(2)}, u32[]{:S(2)}) async-start(f32[2,1024,16,128]{3,2,0,1:T(8,128)} %copy.155), calls=%async_computation.4 | async-start | bytes 33554432 | tf_op jit(solution)/shard_map/all_to_all | solution.py:70
  1127.1 18.6 collective-permute-start.7
  1130.1 49.0 %collective-permute-start.8 = (f32[2,8,128,256]{2,3,1,0:T(8,128)}, f32[2,8,128,256]{2,3,1,0:T(8,128)}, u32[]{:S(2)}, u32[]{:S(2)}) collective-permute-start(f32[2,8,128,256]{2,3,1,0:T(8,128)} %copy.182), channel_id=1, source_target_pairs={{0,8},{4,12},{8,0},{12,4},{16,24},{20,28},{24,16},{28,20},{1,9},{5... | collective-permute-start | bytes 6291464 | tf_op jit(solution)/shard_map/ppermute | solution.py:62
  1135.3 88.4 %collective-permute-start.9 = (f32[2,8,128,256]{2,3,1,0:T(8,128)}, f32[2,8,128,256]{2,3,1,0:T(8,128)}, u32[]{:S(2)}, u32[]{:S(2)}) collective-permute-start(f32[2,8,128,256]{2,3,1,0:T(8,128)} %copy.183), channel_id=1, source_target_pairs={{0,12},{4,8},{8,4},{12,0},{16,28},{20,24},{24,20},{28,16},{1,13},{... | collective-permute-start | bytes 6291464 | tf_op jit(solution)/shard_map/ppermute | solution.py:62
  1138.2 88.6 %collective-permute-start.10 = (f32[2,8,128,256]{2,3,1,0:T(8,128)}, f32[2,8,128,256]{2,3,1,0:T(8,128)}, u32[]{:S(2)}, u32[]{:S(2)}) collective-permute-start(f32[2,8,128,256]{2,3,1,0:T(8,128)} %copy.184), channel_id=1, source_target_pairs={{0,16},{4,20},{8,24},{12,28},{16,0},{20,4},{24,8},{28,12},{1,17},{... | collective-permute-start | bytes 6291464 | tf_op jit(solution)/shard_map/ppermute | solution.py:62
  1142.8 177.6 %collective-permute-start.11 = (f32[2,8,128,256]{2,3,1,0:T(8,128)}, f32[2,8,128,256]{2,3,1,0:T(8,128)}, u32[]{:S(2)}, u32[]{:S(2)}) collective-permute-start(f32[2,8,128,256]{2,3,1,0:T(8,128)} %copy.185), channel_id=1, source_target_pairs={{0,20},{4,16},{8,28},{12,24},{16,4},{20,0},{24,12},{28,8},{1,21},{... | collective-permute-start | bytes 6291464 | tf_op jit(solution)/shard_map/ppermute | solution.py:62
  1145.7 177.7 %collective-permute-start.12 = (f32[2,8,128,256]{2,3,1,0:T(8,128)}, f32[2,8,128,256]{2,3,1,0:T(8,128)}, u32[]{:S(2)}, u32[]{:S(2)}) collective-permute-start(f32[2,8,128,256]{2,3,1,0:T(8,128)} %copy.186), channel_id=1, source_target_pairs={{0,24},{4,28},{8,16},{12,20},{16,8},{20,12},{24,0},{28,4},{1,25},{... | collective-permute-start | bytes 6291464 | tf_op jit(solution)/shard_map/ppermute | solution.py:62
  1179.2 147.4 %collective-permute-start.13 = (f32[2,8,128,256]{2,3,1,0:T(8,128)}, f32[2,8,128,256]{2,3,1,0:T(8,128)}, u32[]{:S(2)}, u32[]{:S(2)}) collective-permute-start(f32[2,8,128,256]{2,3,1,0:T(8,128)} %copy.187), channel_id=1, source_target_pairs={{0,28},{4,24},{8,20},{12,16},{16,12},{20,8},{24,4},{28,0},{1,29},{... | collective-permute-start | bytes 6291464 | tf_op jit(solution)/shard_map/ppermute | solution.py:62
  1537.0 210.7 %all-to-all-start.3 = ((f32[2,64,128,256]{2,3,0,1:T(8,128)}), f32[2,64,128,256]{2,3,0,1:T(8,128)}, u32[]{:S(2)}, u32[]{:S(2)}) async-start(f32[2,64,128,256]{2,3,0,1:T(8,128)} %copy.153), calls=%async_computation.3 | async-start | bytes 33554432 | tf_op jit(solution)/shard_map/all_to_all | solution.py:67
  1561.8 106.1 %copy-start = (f32[1,256,4,16,128]{4,1,3,2,0:T(8,128)}, f32[1,256,4,16,128]{4,1,3,2,0:T(8,128)S(1)}, u32[]{:S(2)}) copy-start(f32[1,256,4,16,128]{4,1,3,2,0:T(8,128)S(1)} %copy.157) | copy-start | bytes 25165828
  1747.6 371.3 %all-to-all-start.5 = ((f32[2,256,64,128]{3,1,0,2:T(8,128)}), f32[2,256,64,128]{3,1,0,2:T(8,128)}, u32[]{:S(2)}, u32[]{:S(2)}) async-start(f32[2,256,64,128]{3,1,0,2:T(8,128)} %copy.169), calls=%async_computation.5 | async-start | bytes 33554432 | tf_op jit(solution)/shard_map/all_to_all | solution.py:72
  (13 other events, 434.4 us)
